TPU v7x, 512 devices: a whole 4x8x8 slice. The times are simulated.
512 devices in a mesh: rep: 64 (over y, x, core), ch: 8 (over z).
Axes of the slice: x: 4, y: 8, z: 8, core: 2. Of those that a mesh axis runs over, the one named last changes fastest.
Arguments:
- inputs: float32 [128, 14, 14, 512], P('rep'), may hold values from -6 to 6
- grad_out: float32 [128, 14, 14, 1024], P('rep', None, None, 'ch'), may hold values from -81 to 81
- weight: float32 [1024, 3, 3, 512], P('ch'), may hold values from -0.09375 to 0.09375
- momentum: float32 [1024, 3, 3, 512], P(('ch', 'rep')), may hold values from -6 to 6
Outputs:
- input_grad: float32 [128, 14, 14, 512], P('rep', None, None, 'ch')
- new_weight: float32 [1024, 3, 3, 512], P(('ch', 'rep'))
- new_momentum: float32 [1024, 3, 3, 512], P(('ch', 'rep'))
All inputs are finite; a program needn't handle non-finite values.
Results may differ from a plain program's by a relative error of at most 0.0001.
Values sent between devices are 32-bit elements; how exact they have to be, the bound alone decides.
No kernel may reach another device: no remote copies, remote signals or barrier semaphores. Data moves between devices by JAX's collectives and lax.ppermute only.
A program may use at most 64 MiB of HBM per device.

v0:
```python
import math

import jax
import jax.numpy as jnp
from jax import lax
from jax.sharding import PartitionSpec as P

CO = 1024
CI = 512


EPSILON = 1e-06
MOMENTUM_RATE = 0.9
LEARN_RATE = 0.05


def partner(value, axis, bit):
    mask = 2**bit
    pairs = [(source, source ^ mask) for source in range(lax.axis_size(axis))]
    return lax.ppermute(value, axis, pairs)


def pair_combine(left_term, right_term):
    cross_dot = jnp.sum(left_term * right_term, axis=-1, keepdims=True)
    left_sq = jnp.sum(left_term * left_term, axis=-1, keepdims=True)
    right_sq = jnp.sum(right_term * right_term, axis=-1, keepdims=True)
    return (1.0 - cross_dot / (2.0 * (left_sq + EPSILON))) * left_term + (
        1.0 - cross_dot / (2.0 * (right_sq + EPSILON))
    ) * right_term


def filter_grads(inputs, grad_out):
    images, height, across, chan_in = inputs.shape
    chan_out = grad_out.shape[3]
    padded = jnp.pad(inputs, ((0, 0), (1, 1), (1, 1), (0, 0)))
    grad_rows = grad_out.reshape(images * height * across, chan_out)
    tap_list = []
    for tap_row in range(3):
        for tap_col in range(3):
            window = padded[:, tap_row : tap_row + height, tap_col : tap_col + across, :].reshape(
                images * height * across, chan_in
            )
            tap_list.append(
                lax.dot_general(
                    grad_rows,
                    window,
                    (((0,), (0,)), ((), ())),
                    precision=lax.Precision.HIGHEST,
                    preferred_element_type=jnp.float32,
                )
            )
    return jnp.stack(tap_list, axis=1).reshape(chan_out, 9 * chan_in)


def input_grads(grad_out, weight):
    images, height, across, chan_out = grad_out.shape
    padded = jnp.pad(grad_out, ((0, 0), (1, 1), (1, 1), (0, 0)))
    summed = jnp.zeros((images * height * across, weight.shape[3]), jnp.float32)
    for tap_row in range(3):
        for tap_col in range(3):
            window = padded[
                :, 2 - tap_row : 2 - tap_row + height, 2 - tap_col : 2 - tap_col + across, :
            ].reshape(images * height * across, chan_out)
            summed = summed + jnp.dot(
                window,
                weight[:, tap_row, tap_col, :],
                precision=lax.Precision.HIGHEST,
                preferred_element_type=jnp.float32,
            )
    return summed


def local(inputs, grad_out, weight, momentum):
    images, height, across, chan_in = inputs.shape
    chan_out = grad_out.shape[3]
    replicas = lax.axis_size("rep")
    col_count = chan_in // lax.axis_size("ch")
    own_count = chan_out // replicas
    rep_index = lax.axis_index("rep")
    local_grads = filter_grads(inputs, grad_out)
    current = local_grads
    levels = replicas.bit_length() - 1
    for section in range(levels):
        bit_pos = levels - 1 - section
        half_rows = current.shape[0] // 2
        lower_rows = current[:half_rows]
        upper_rows = current[half_rows:]
        bit_zero = rep_index // (1 << bit_pos) % 2 == 0
        kept_rows = jnp.where(bit_zero, lower_rows, upper_rows)
        sent_rows = jnp.where(bit_zero, upper_rows, lower_rows)
        received = partner(sent_rows, "rep", bit_pos)
        current = pair_combine(kept_rows, received)
    flat_grad = input_grads(grad_out, weight)
    scattered = lax.psum_scatter(
        flat_grad.reshape(images * height * across, 1 * lax.axis_size("ch"), col_count).transpose(
            1, 0, 2
        ),
        "ch",
        scatter_dimension=0,
        tiled=True,
    )
    input_grad = scattered.reshape(images, height, across, col_count)
    norm_sq = lax.psum(jnp.sum(current * current), ("rep", "ch"))
    clip_scale = jnp.minimum(1.0, 0.5 * math.sqrt(CO * 9 * CI) / jnp.sqrt(norm_sq + EPSILON))
    owned_w = lax.dynamic_slice_in_dim(weight, rep_index * own_count, own_count, 0)
    new_momentum = MOMENTUM_RATE * momentum + clip_scale * current.reshape(own_count, 3, 3, chan_in)
    new_weight = owned_w - LEARN_RATE * new_momentum
    return (input_grad, new_weight, new_momentum)


def solution(mesh):
    in_specs = (
        P("rep", None, None, None),
        P("rep", None, None, "ch"),
        P("ch", None, None, None),
        P(("ch", "rep"), None, None, None),
    )
    out_specs = (
        P("rep", None, None, "ch"),
        P(("ch", "rep"), None, None, None),
        P(("ch", "rep"), None, None, None),
    )
    return jax.shard_map(local, mesh=mesh, in_specs=in_specs, out_specs=out_specs, check_vma=False)
```

profile of v0, /device:TPU:1, one launch (start us, length us, event | category | flops | bytes accessed | tf_op | source)
XLA Modules:
  0.0 292.8 jit_solution(8104192545657644004)
XLA Ops:
  7.3 1.4 copy.57
  8.6 1.9 fusion.8
  10.5 0.9 fusion.7
  11.4 1.0 fusion.6
  12.4 1.0 fusion.5
  13.3 0.9 fusion.4
  14.2 1.0 fusion.3
  15.2 0.9 fusion.2
  16.1 0.9 fusion.1
  17.0 0.9 fusion
  18.3 1.1 copy.84
  19.4 8.3 %collective-permute-start = (f32[64,4608]{1,0:T(8,128)}, f32[64,4608]{1,0:T(8,128)}, u32[]{:S(2)}, u32[]{:S(2)}) collective-permute-start(f32[64,4608]{1,0:T(8,128)} %bitcast.76), channel_id=1, source_target_pairs={{0,256},{8,264},{16,272},{24,280},{32,288},{40,296},{48,304},{56,3... | collective-permute-start | bytes 3538952 | tf_op jit(solution)/shard_map/ppermute | solution.py:20
  27.8 1.2 pad_slice_fusion.16
  29.2 0.7 reshape.205
  29.9 1.7 fusion.18
  31.6 1.8 convolution_add_fusion.7
  33.4 33.7 %collective-permute-done = f32[64,4608]{1,0:T(8,128)} collective-permute-done((f32[64,4608]{1,0:T(8,128)}, f32[64,4608]{1,0:T(8,128)}, u32[]{:S(2)}, u32[]{:S(2)}) %collective-permute-start) | collective-permute-done | bytes 1179680 | tf_op jit(solution)/shard_map/ppermute | solution.py:20
  67.0 1.5 multiply_reduce_fusion
  68.6 1.5 multiply_add_fusion
  70.1 0.9 slice_select_fusion.1
  71.0 16.9 %collective-permute-start.1 = (f32[32,4608]{1,0:T(8,128)}, f32[32,4608]{1,0:T(8,128)S(1)}, u32[]{:S(2)}, u32[]{:S(2)}) collective-permute-start(f32[32,4608]{1,0:T(8,128)} %slice_select_fusion.1), channel_id=1, source_target_pairs={{0,128},{8,136},{16,144},{24,152},{32,160},{40,168},{48,176},{56,1... | collective-permute-start | bytes 1769480 | tf_op jit(solution)/shard_map/ppermute | solution.py:20
  87.9 1.8 convolution_add_fusion.6
  89.7 1.0 copy.47
  90.7 0.7 reshape.207
  91.4 1.0 copy.49
  92.4 1.7 convolution_add_fusion.5
  94.1 1.9 convolution_add_fusion.4
  96.0 18.3 %collective-permute-done.1 = f32[32,4608]{1,0:T(8,128)S(1)} collective-permute-done((f32[32,4608]{1,0:T(8,128)}, f32[32,4608]{1,0:T(8,128)S(1)}, u32[]{:S(2)}, u32[]{:S(2)}) %collective-permute-start.1) | collective-permute-done | bytes 589856 | tf_op jit(solution)/shard_map/ppermute | solution.py:20
  114.7 0.7 slice_select_fusion.3
  115.4 1.9 collective-permute-start.2
  117.4 1.7 convolution_add_fusion.3
  119.4 1.7 convolution_add_fusion.2
  121.1 4.5 %collective-permute-done.2 = f32[16,4608]{1,0:T(8,128)S(1)} collective-permute-done((f32[16,4608]{1,0:T(8,128)}, f32[16,4608]{1,0:T(8,128)S(1)}, u32[]{:S(2)}, u32[]{:S(2)}) %collective-permute-start.2) | collective-permute-done | bytes 294944 | tf_op jit(solution)/shard_map/ppermute | solution.py:20
  125.9 4.8 %collective-permute-start.3 = (f32[8,4608]{1,0:T(8,128)S(1)}, f32[8,4608]{1,0:T(8,128)S(1)}, u32[]{:S(2)}, u32[]{:S(2)}) collective-permute-start(f32[8,4608]{1,0:T(8,128)S(1)} %slice_select_fusion.5), channel_id=1, source_target_pairs={{0,32},{8,40},{16,48},{24,56},{32,0},{40,8},{48,16},{56,24},{64,96... | collective-permute-start | bytes 442376 | tf_op jit(solution)/shard_map/ppermute | solution.py:20
  130.8 1.7 convolution_add_fusion.1
  132.5 0.8 collective-permute-done.3
  133.7 3.2 %collective-permute-start.4 = (f32[4,4608]{1,0:T(4,128)S(1)}, f32[4,4608]{1,0:T(4,128)S(1)}, u32[]{:S(2)}, u32[]{:S(2)}) collective-permute-start(f32[4,4608]{1,0:T(4,128)S(1)} %slice_select_fusion.7), channel_id=1, source_target_pairs={{0,16},{8,24},{16,0},{24,8},{32,48},{40,56},{48,32},{56,40},{64,80... | collective-permute-start | bytes 221192 | tf_op jit(solution)/shard_map/ppermute | solution.py:20
  136.9 1.8 convolution_add_fusion
  138.7 1.3 copy.53
  140.4 4.7 %collective-permute-start.5 = (f32[2,4608]{1,0:T(2,128)S(1)}, f32[2,4608]{1,0:T(2,128)S(1)}, u32[]{:S(2)}, u32[]{:S(2)}) collective-permute-start(f32[2,4608]{1,0:T(2,128)S(1)} %broadcast_select_fusion), channel_id=1, source_target_pairs={{0,8},{8,0},{16,24},{24,16},{32,40},{40,32},{48,56},{56,48},{64,72... | collective-permute-start | bytes 110600 | tf_op jit(solution)/shard_map/ppermute | solution.py:20
  145.1 0.9 constant_dynamic-slice_fusion
  146.0 34.4 %reduce-scatter.2.cloned.1.call-done = f32[1,392,64]{1,2,0:T(8,128)} async-done(((f32[8,392,64]{1,2,0:T(8,128)}), f32[1,392,64]{1,2,0:T(8,128)}) %reduce-scatter.2.cloned.1.call-update) | async-done | bytes 100368 | tf_op jit(solution)/shard_map/reduce_scatter | solution.py:94
  180.4 1.0 copy.54
  181.5 0.8 copy.70
  182.5 0.7 multiply_reduce_fusion.15
  183.3 100.6 %psum.7 = f32[]{:T(128)} all-reduce(f32[]{:T(128)} %get-tuple-element.28), channel_id=1, replica_groups=mesh['rep'=64,'ch'=8] {'rep','ch'}, use_global_device_ids=true, to_apply=%region_20.21 | all-reduce | flops 1 | bytes 8 | tf_op jit(solution)/shard_map/psum | solution.py:103
  284.7 0.6 copy.71
  285.3 0.6 copy.72
  (54 shorter events, 2.6 us)
Async XLA Ops:
  7.2 3.3 %copy-start = (f32[2,14,14,128]{3,0,2,1:T(2,128)S(1)}, f32[2,14,14,128]{3,0,2,1:T(2,128)}, u32[]{:S(2)}) copy-start(f32[2,14,14,128]{3,0,2,1:T(2,128)} %param.5) | copy-start | bytes 602116
  7.2 173.3 %reduce-scatter.2.cloned.1.call-start = ((), (), s32[]{:S(2)}) async-start(), calls=%async_computation.1 | async-start | bytes 1179648 | tf_op jit(solution)/shard_map/reduce_scatter | solution.py:94
  10.5 2.8 copy-start.1
  19.4 47.6 %collective-permute-start = (f32[64,4608]{1,0:T(8,128)}, f32[64,4608]{1,0:T(8,128)}, u32[]{:S(2)}, u32[]{:S(2)}) collective-permute-start(f32[64,4608]{1,0:T(8,128)} %bitcast.76), channel_id=1, source_target_pairs={{0,256},{8,264},{16,272},{24,280},{32,288},{40,296},{48,304},{56,3... | collective-permute-start | bytes 3538952 | tf_op jit(solution)/shard_map/ppermute | solution.py:20
  68.6 19.3 %copy-start.4 = (f32[392,128]{1,0:T(8,128)S(1)}, f32[392,128]{1,0:T(8,128)}, u32[]{:S(2)}) copy-start(f32[392,128]{1,0:T(8,128)} %reshape.205) | copy-start | bytes 602116
  71.0 43.3 %collective-permute-start.1 = (f32[32,4608]{1,0:T(8,128)}, f32[32,4608]{1,0:T(8,128)S(1)}, u32[]{:S(2)}, u32[]{:S(2)}) collective-permute-start(f32[32,4608]{1,0:T(8,128)} %slice_select_fusion.1), channel_id=1, source_target_pairs={{0,128},{8,136},{16,144},{24,152},{32,160},{40,168},{48,176},{56,1... | collective-permute-start | bytes 1769480 | tf_op jit(solution)/shard_map/ppermute | solution.py:20
  114.5 4.6 %copy-start.3 = (f32[2,14,14,128]{3,0,2,1:T(2,128)S(1)}, f32[2,14,14,128]{3,0,2,1:T(2,128)}, u32[]{:S(2)}) copy-start(f32[2,14,14,128]{3,0,2,1:T(2,128)} %get-tuple-element.43) | copy-start | bytes 602116
  114.7 4.5 %copy-start.2 = (f32[2,14,14,128]{3,0,2,1:T(2,128)S(1)}, f32[2,14,14,128]{3,0,2,1:T(2,128)}, u32[]{:S(2)}) copy-start(f32[2,14,14,128]{3,0,2,1:T(2,128)} %get-tuple-element.44) | copy-start | bytes 602116
  115.4 10.1 %collective-permute-start.2 = (f32[16,4608]{1,0:T(8,128)}, f32[16,4608]{1,0:T(8,128)S(1)}, u32[]{:S(2)}, u32[]{:S(2)}) collective-permute-start(f32[16,4608]{1,0:T(8,128)} %slice_select_fusion.3), channel_id=1, source_target_pairs={{0,64},{8,72},{16,80},{24,88},{32,96},{40,104},{48,112},{56,120},{... | collective-permute-start | bytes 884744 | tf_op jit(solution)/shard_map/ppermute | solution.py:20
  125.9 7.4 %collective-permute-start.3 = (f32[8,4608]{1,0:T(8,128)S(1)}, f32[8,4608]{1,0:T(8,128)S(1)}, u32[]{:S(2)}, u32[]{:S(2)}) collective-permute-start(f32[8,4608]{1,0:T(8,128)S(1)} %slice_select_fusion.5), channel_id=1, source_target_pairs={{0,32},{8,40},{16,48},{24,56},{32,0},{40,8},{48,16},{56,24},{64,96... | collective-permute-start | bytes 442376 | tf_op jit(solution)/shard_map/ppermute | solution.py:20
  133.7 6.4 %collective-permute-start.4 = (f32[4,4608]{1,0:T(4,128)S(1)}, f32[4,4608]{1,0:T(4,128)S(1)}, u32[]{:S(2)}, u32[]{:S(2)}) collective-permute-start(f32[4,4608]{1,0:T(4,128)S(1)} %slice_select_fusion.7), channel_id=1, source_target_pairs={{0,16},{8,24},{16,0},{24,8},{32,48},{40,56},{48,32},{56,40},{64,80... | collective-permute-start | bytes 221192 | tf_op jit(solution)/shard_map/ppermute | solution.py:20
  138.7 146.0 %copy-start.5 = (f32[2,3,3,512]{3,0,2,1:T(2,128)S(1)}, f32[2,3,3,512]{3,0,2,1:T(2,128)}, u32[]{:S(2)}) copy-start(f32[2,3,3,512]{3,0,2,1:T(2,128)} %param.7) | copy-start | bytes 110596
  140.4 41.9 %collective-permute-start.5 = (f32[2,4608]{1,0:T(2,128)S(1)}, f32[2,4608]{1,0:T(2,128)S(1)}, u32[]{:S(2)}, u32[]{:S(2)}) collective-permute-start(f32[2,4608]{1,0:T(2,128)S(1)} %broadcast_select_fusion), channel_id=1, source_target_pairs={{0,8},{8,0},{16,24},{24,16},{32,40},{40,32},{48,56},{56,48},{64,72... | collective-permute-start | bytes 110600 | tf_op jit(solution)/shard_map/ppermute | solution.py:20
Sparse Core Ops, SparseCore 0:
  140.2 40.2 reduce-scatter.1
where the time goes:
time: 294 us; the launch traced here: 293 us
  blocking collectives  101 us (34%)
  waiting for transfers between devices  91.7 us (31%)
  starting transfers between devices  39.8 us (14%)
  matrix products  25.1 us (9%)
  between operations  15.4 us (5%)
  local copies, waits for them, and re-layouts  12.8 us (4%)
  other arithmetic  7.42 us (3%)
    psum x1, blocking collectives, local(): norm_sq = lax.psum(jnp.sum(current * current), ('rep', 'ch'))  101 us
    ppermute x6, waiting for transfers between devices, partner(): return lax.ppermute(value, axis, pairs)  57.3 us
    ppermute x6, starting transfers between devices, partner(): return lax.ppermute(value, axis, pairs)  39.8 us
    reduce_scatter x1, waiting for transfers between devices, local(): lax.psum_scatter(flat_grad.reshape(images * height * across, 1 * lax.axis...  34.4 us
    dot_general x9, matrix products, input_grads(): jnp.dot(window, weight[:, tap_row, tap_col, :], precision=lax.Precision.H...  15.8 us
    dot_general x9, matrix products, filter_grads(): lax.dot_general(grad_rows, window, (((0,), (0,)), ((), ())), precision=la...  9.26 us
  transfers between devices with their start and end apart: 7, of which 5 were waited for; matrix products, arithmetic and copies ran while one was open for 9% of the time, Pallas kernels for 0%

commit v1 on v0

v1 whole, which is shorter than its diff:
```python
import math

import jax
import jax.numpy as jnp
from jax import lax
from jax.sharding import PartitionSpec as P

CO = 1024
CI = 512


EPSILON = 1e-06
MOMENTUM_RATE = 0.9
LEARN_RATE = 0.05
PREC = lax.Precision.HIGH


def filter_grads(inputs, grad_out):
    images, height, across, chan_in = inputs.shape
    chan_out = grad_out.shape[3]
    padded = jnp.pad(inputs, ((0, 0), (1, 1), (1, 1), (0, 0)))
    grad_rows = grad_out.reshape(images * height * across, chan_out)
    tap_list = []
    for tap_row in range(3):
        for tap_col in range(3):
            window = padded[:, tap_row : tap_row + height, tap_col : tap_col + across, :].reshape(
                images * height * across, chan_in
            )
            tap_list.append(
                lax.dot_general(
                    grad_rows,
                    window,
                    (((0,), (0,)), ((), ())),
                    precision=PREC,
                    preferred_element_type=jnp.float32,
                )
            )
    return jnp.stack(tap_list, axis=1)


def input_grads(grad_out, weight):
    images, height, across, chan_out = grad_out.shape
    padded = jnp.pad(grad_out, ((0, 0), (1, 1), (1, 1), (0, 0)))
    summed = jnp.zeros((images * height * across, weight.shape[3]), jnp.float32)
    for tap_row in range(3):
        for tap_col in range(3):
            window = padded[
                :, 2 - tap_row : 2 - tap_row + height, 2 - tap_col : 2 - tap_col + across, :
            ].reshape(images * height * across, chan_out)
            summed = summed + jnp.dot(
                window,
                weight[:, tap_row, tap_col, :],
                precision=PREC,
                preferred_element_type=jnp.float32,
            )
    return summed


def row_sums(value):
    rows = jnp.sum(value, axis=(1, 3))
    per = jnp.sum(rows.reshape(-1, 2, 4), axis=2, keepdims=True)
    return jnp.broadcast_to(per, per.shape[:2] + (4,)).reshape(-1, 1, 8, 1)


def pair_combine(left_term, right_term):
    cross_dot = row_sums(left_term * right_term)
    left_sq = row_sums(left_term * left_term)
    right_sq = row_sums(right_term * right_term)
    return (1.0 - cross_dot / (2.0 * (left_sq + EPSILON))) * left_term + (
        1.0 - cross_dot / (2.0 * (right_sq + EPSILON))
    ) * right_term


def global_sum(value, axes):
    for axis in axes:
        size = lax.axis_size(axis)
        spread = jnp.broadcast_to(value, (size, 1, 128))
        spread = lax.all_to_all(spread, axis, 0, 0, tiled=True)
        value = jnp.sum(spread[:, 0, 0])
    return value


def local(inputs, grad_out, weight, momentum):
    images, height, across, chan_in = inputs.shape
    chan_out = grad_out.shape[3]
    replicas = lax.axis_size("rep")
    planes = lax.axis_size("ch")
    col_count = chan_in // planes
    own_count = chan_out // replicas
    rep_index = lax.axis_index("rep")
    grads = filter_grads(inputs, grad_out)
    sent = (
        grads.reshape(replicas, own_count, 9, chan_in // 128, 128)
        .transpose(0, 2, 1, 3, 4)
        .reshape(replicas, 9, 8, 128)
    )
    current = lax.all_to_all(sent, "rep", 0, 0, tiled=True)

    flat_grad = input_grads(grad_out, weight)
    half = height * across
    parts = (
        flat_grad.reshape(images, half, planes, col_count)
        .transpose(2, 1, 0, 3)
        .reshape(planes, half, images * col_count)
    )
    parts = lax.all_to_all(parts, "ch", 0, 0, tiled=True)
    input_grad = (
        jnp.sum(parts, axis=0)
        .reshape(half, images, col_count)
        .transpose(1, 0, 2)
        .reshape(images, height, across, col_count)
    )

    while current.shape[0] > 1:
        upper = current.shape[0] // 2
        current = pair_combine(current[:upper], current[upper:])
    combined = (
        current.reshape(9, own_count, chan_in // 128, 128)
        .transpose(1, 0, 2, 3)
        .reshape(own_count, 3, 3, chan_in)
    )
    norm_sq = global_sum(jnp.sum(current * current), ("rep", "ch"))
    clip_scale = jnp.minimum(1.0, 0.5 * math.sqrt(CO * 9 * CI) / jnp.sqrt(norm_sq + EPSILON))
    owned_w = lax.dynamic_slice_in_dim(weight, rep_index * own_count, own_count, 0)
    new_momentum = MOMENTUM_RATE * momentum + clip_scale * combined
    new_weight = owned_w - LEARN_RATE * new_momentum
    return (input_grad, new_weight, new_momentum)


def solution(mesh):
    in_specs = (
        P("rep", None, None, None),
        P("rep", None, None, "ch"),
        P("ch", None, None, None),
        P(("ch", "rep"), None, None, None),
    )
    out_specs = (
        P("rep", None, None, "ch"),
        P(("ch", "rep"), None, None, None),
        P(("ch", "rep"), None, None, None),
    )
    return jax.shard_map(local, mesh=mesh, in_specs=in_specs, out_specs=out_specs, check_vma=False)
```

time: 294 us -> 181 us (0.62)
  blocking collectives: 101 us -> 0 us
  local copies, waits for them, and re-layouts: 12.8 us -> 45.7 us
  waiting for transfers between devices: 91.7 us -> 70.8 us
  between operations: 15.4 us -> 1.95 us
  starting transfers between devices: 39.8 us -> 31.9 us
    psum x1 -> x0, blocking collectives: 101 us -> none  [local(): norm_sq = lax.psum(jnp.sum(current * current), ('rep', 'ch'))]
    all_to_all x0 -> x4, waiting for transfers between devices: none -> 70.8 us  [the longest x1 36.6 us: local(): current = lax.all_to_all(sent, 'rep', 0, 0, tiled=True)]
    ppermute x6 -> x0, waiting for transfers between devices: 57.3 us -> none  [partner(): return lax.ppermute(value, axis, pairs)]
    ppermute x6 -> x0, starting transfers between devices: 39.8 us -> none  [partner(): return lax.ppermute(value, axis, pairs)]
    reduce_scatter x1 -> x0, waiting for transfers between devices: 34.4 us -> none  [local(): lax.psum_scatter(flat_grad.reshape(images * height * across, 1 * lax.axis...]
    all_to_all x0 -> x4, starting transfers between devices: none -> 31.9 us  [the longest x1 11.6 us: local(): current = lax.all_to_all(sent, 'rep', 0, 0, tiled=True)]
    dot_general x0 -> x8, local copies, waits for them, and re-layouts: none -> 9.61 us  [filter_grads(): lax.dot_general(grad_rows, window, (((0,), (0,)), ((), ())), precision=PR...]
    another operation x0 -> x10, local copies, waits for them, and re-layouts: none -> 9.09 us  [filter_grads(): return jnp.stack(tap_list, axis=1)]
  transfers between devices with their start and end apart: 7 -> 4, of which waited for: 5 -> 4; matrix products, arithmetic and copies ran while one was open for 9% -> 13% of each run, Pallas kernels for 0% -> 0%
where the time goes in v1:
time: 181 us; the launch traced here: 180 us
  waiting for transfers between devices  70.8 us (39%)
  local copies, waits for them, and re-layouts  45.7 us (25%)
  starting transfers between devices  31.9 us (18%)
  matrix products  22.8 us (13%)
  other arithmetic  6.85 us (4%)
  between operations  1.95 us (1%)
    all_to_all x1, waiting for transfers between devices, local(): current = lax.all_to_all(sent, 'rep', 0, 0, tiled=True)  36.6 us
    all_to_all x1, waiting for transfers between devices, local(): parts = lax.all_to_all(parts, 'ch', 0, 0, tiled=True)  23.6 us
    dot_general x9, matrix products, filter_grads(): lax.dot_general(grad_rows, window, (((0,), (0,)), ((), ())), precision=PR...  14.5 us
    all_to_all x1, starting transfers between devices, local(): current = lax.all_to_all(sent, 'rep', 0, 0, tiled=True)  11.6 us
    all_to_all x2, waiting for transfers between devices, global_sum(): spread = lax.all_to_all(spread, axis, 0, 0, tiled=True)  10.6 us
    all_to_all x2, starting transfers between devices, global_sum(): spread = lax.all_to_all(spread, axis, 0, 0, tiled=True)  10.2 us
    all_to_all x1, starting transfers between devices, local(): parts = lax.all_to_all(parts, 'ch', 0, 0, tiled=True)  10 us
    dot_general x8, local copies, waits for them, and re-layouts, filter_grads(): lax.dot_general(grad_rows, window, (((0,), (0,)), ((), ())), precision=PR...  9.61 us
  transfers between devices with their start and end apart: 4, of which 4 were waited for; matrix products, arithmetic and copies ran while one was open for 13% of the time, Pallas kernels for 0%

profile of v1, /device:TPU:1, one launch (start us, length us, event | category | flops | bytes accessed | tf_op | source)
XLA Modules:
  0.0 179.9 jit_solution(10587074147059767241)
XLA Ops:
  0.6 1.4 copy.285
  2.0 1.9 %convolution_bitcast_fusion.8 = f32[128,512]{0,1:T(8,128)S(1)} fusion(f32[2,14,14,512]{3,2,1,0:T(8,128)S(1)} %copy.285, f32[2,14,14,128]{3,0,2,1:T(2,128)} %param.5), kind=kOutput, calls=%fused_computation.20 | convolution fusion | flops 154140672 | bytes 1265664 | tf_op jit(solution)/shard_map/dot_general | solution.py:30
  4.0 1.0 convolution_bitcast_fusion.7
  5.0 1.7 convolution_bitcast_fusion.6
  6.7 1.7 convolution_bitcast_fusion.5
  8.4 1.3 convolution_bitcast_fusion.4
  9.7 1.7 convolution_bitcast_fusion.3
  11.4 1.7 convolution_bitcast_fusion.2
  13.2 1.7 convolution_bitcast_fusion.1
  14.9 1.7 convolution_bitcast_fusion
  17.1 1.1 copy.291
  18.3 1.1 copy.293
  20.1 1.0 stack.34
  21.2 1.8 %copy.297 = f32[128,512]{1,0:T(8,128)} copy(f32[128,512]{0,1:T(8,128)} %convolution_bitcast_fusion.3) | data formatting | bytes 524288 | tf_op jit(solution)/shard_map/dot_general | solution.py:30
  23.0 1.7 stack.35
  24.7 1.8 copy.299
  26.5 1.8 stack.36
  28.3 1.8 copy.301
  30.1 1.7 stack.37
  31.8 1.8 copy.303
  33.6 1.7 stack.38
  35.4 1.0 constant_dynamic-update-slice_fusion.5
  36.5 1.0 constant_dynamic-update-slice_fusion.3
  37.7 1.6 copy.305
  39.2 11.6 %all-to-all-start.1 = ((f32[64,9,8,128]{3,2,1,0:T(8,128)}), f32[64,9,8,128]{3,2,1,0:T(8,128)S(1)}, u32[]{:S(2)}, u32[]{:S(2)}) async-start(f32[64,9,8,128]{3,2,1,0:T(8,128)} %copy.305), calls=%async_computation.1 | async-start | bytes 4718592 | tf_op jit(solution)/shard_map/all_to_all | solution.py:97
  50.9 1.3 pad_slice_fusion.16
  52.2 1.0 copy.272
  53.9 1.0 copy.273
  57.0 1.0 copy.276
  58.7 1.0 copy.277
  60.3 1.0 copy.278
  62.7 1.6 fusion.8
  64.3 1.5 convolution_add_fusion.7
  68.2 1.4 convolution_add_fusion.1
  69.6 36.6 %all-to-all-done.1 = f32[64,9,8,128]{3,2,1,0:T(8,128)S(1)} async-done(((f32[64,9,8,128]{3,2,1,0:T(8,128)}), f32[64,9,8,128]{3,2,1,0:T(8,128)S(1)}, u32[]{:S(2)}, u32[]{:S(2)}) %all-to-all-start.1) | async-done | bytes 2359328 | tf_op jit(solution)/shard_map/all_to_all | solution.py:97
  107.6 0.9 multiply_add_fusion
  114.1 1.3 broadcast_in_dim.40
  115.4 6.9 %all-to-all-start.2 = ((f32[64,1,128]{2,1,0:T(1,128)}), f32[64,1,128]{2,1,0:T(1,128)S(1)}, u32[]{:S(2)}, u32[]{:S(2)}) async-start(f32[64,1,128]{2,1,0:T(1,128)} %broadcast_in_dim.40), calls=%async_computation.2 | async-start | bytes 65536 | tf_op jit(solution)/shard_map/all_to_all | solution.py:78
  122.3 1.5 convolution_add_fusion
  124.2 0.9 reshape.516
  125.2 1.2 copy.282
  126.4 5.2 %all-to-all-done.2 = f32[64,1,128]{2,1,0:T(1,128)S(1)} async-done(((f32[64,1,128]{2,1,0:T(1,128)}), f32[64,1,128]{2,1,0:T(1,128)S(1)}, u32[]{:S(2)}, u32[]{:S(2)}) %all-to-all-start.2) | async-done | bytes 32800 | tf_op jit(solution)/shard_map/all_to_all | solution.py:78
  131.6 10.0 %all-to-all-start = ((f32[8,196,128]{2,1,0:T(8,128)}), f32[8,196,128]{2,1,0:T(8,128)S(1)}, u32[]{:S(2)}, u32[]{:S(2)}) async-start(f32[8,196,128]{2,1,0:T(8,128)} %copy.282), calls=%async_computation | async-start | bytes 1638400 | tf_op jit(solution)/shard_map/all_to_all | solution.py:106
  142.3 23.6 %all-to-all-done = f32[8,196,128]{2,1,0:T(8,128)S(1)} async-done(((f32[8,196,128]{2,1,0:T(8,128)}), f32[8,196,128]{2,1,0:T(8,128)S(1)}, u32[]{:S(2)}, u32[]{:S(2)}) %all-to-all-start) | async-done | bytes 802848 | tf_op jit(solution)/shard_map/all_to_all | solution.py:106
  166.0 1.2 broadcast_in_dim.41
  167.2 3.3 %all-to-all-start.3 = ((f32[8,1,128]{2,1,0:T(1,128)}), f32[8,1,128]{2,1,0:T(1,128)S(1)}, u32[]{:S(2)}, u32[]{:S(2)}) async-start(f32[8,1,128]{2,1,0:T(1,128)} %broadcast_in_dim.41), calls=%async_computation.3 | async-start | bytes 8192 | tf_op jit(solution)/shard_map/all_to_all | solution.py:78
  171.5 5.4 %all-to-all-done.3 = f32[8,1,128]{2,1,0:T(1,128)S(1)} async-done(((f32[8,1,128]{2,1,0:T(1,128)}), f32[8,1,128]{2,1,0:T(1,128)S(1)}, u32[]{:S(2)}, u32[]{:S(2)}) %all-to-all-start.3) | async-done | bytes 4128 | tf_op jit(solution)/shard_map/all_to_all | solution.py:78
  178.3 1.6 multiply_subtract_fusion
  (157 shorter events, 19.3 us)
Async XLA Ops:
  0.6 3.3 %copy-start.3 = (f32[2,14,14,128]{3,0,2,1:T(2,128)S(1)}, f32[2,14,14,128]{3,0,2,1:T(2,128)}, u32[]{:S(2)}) copy-start(f32[2,14,14,128]{3,0,2,1:T(2,128)} %param.5) | copy-start | bytes 602116
  6.7 1.7 copy-start
  35.3 2.2 %copy-start.4 = (f32[64,2,1,4,128]{4,3,1,0,2:T(4,128)S(1)}, f32[64,2,1,4,128]{4,3,1,0,2:T(4,128)}, u32[]{:S(2)}) copy-start(f32[64,2,1,4,128]{4,3,1,0,2:T(4,128)} %stack.36) | copy-start | bytes 786436
  35.3 2.2 %copy-start.5 = (f32[64,2,1,4,128]{4,3,1,0,2:T(4,128)S(1)}, f32[64,2,1,4,128]{4,3,1,0,2:T(4,128)}, u32[]{:S(2)}) copy-start(f32[64,2,1,4,128]{4,3,1,0,2:T(4,128)} %stack.37) | copy-start | bytes 786436
  35.3 2.3 %copy-start.6 = (f32[64,2,1,4,128]{4,3,1,0,2:T(4,128)S(1)}, f32[64,2,1,4,128]{4,3,1,0,2:T(4,128)}, u32[]{:S(2)}) copy-start(f32[64,2,1,4,128]{4,3,1,0,2:T(4,128)} %stack.38) | copy-start | bytes 786436
  39.2 67.0 %all-to-all-start.1 = ((f32[64,9,8,128]{3,2,1,0:T(8,128)}), f32[64,9,8,128]{3,2,1,0:T(8,128)S(1)}, u32[]{:S(2)}, u32[]{:S(2)}) async-start(f32[64,9,8,128]{3,2,1,0:T(8,128)} %copy.305), calls=%async_computation.1 | async-start | bytes 4718592 | tf_op jit(solution)/shard_map/all_to_all | solution.py:97
  52.2 3.4 %copy-start.7 = (f32[2,14,14,128]{3,0,2,1:T(2,128)S(1)}, f32[2,14,14,128]{3,0,2,1:T(2,128)}, u32[]{:S(2)}) copy-start(f32[2,14,14,128]{3,0,2,1:T(2,128)} %get-tuple-element.29) | copy-start | bytes 602116
  57.0 7.3 %copy-start.9 = (f32[392,128]{1,0:T(8,128)S(1)}, f32[392,128]{1,0:T(8,128)}, u32[]{:S(2)}) copy-start(f32[392,128]{1,0:T(8,128)} %reshape.508) | copy-start | bytes 602116
  61.3 4.5 %copy-start.10 = (f32[392,128]{1,0:T(8,128)S(1)}, f32[392,128]{1,0:T(8,128)}, u32[]{:S(2)}) copy-start(f32[392,128]{1,0:T(8,128)} %reshape.509) | copy-start | bytes 602116
  62.7 3.1 %copy-start.2 = (f32[128,3,3,512]{3,0,2,1:T(8,128)S(1)}, f32[128,3,3,512]{3,0,2,1:T(8,128)}, u32[]{:S(2)}) copy-start(f32[128,3,3,512]{3,0,2,1:T(8,128)} %param.6) | copy-start | bytes 7077892
  64.3 2.0 %copy-start.12 = (f32[392,128]{1,0:T(8,128)S(1)}, f32[392,128]{1,0:T(8,128)}, u32[]{:S(2)}) copy-start(f32[392,128]{1,0:T(8,128)} %reshape.510) | copy-start | bytes 602116
  65.8 1.0 copy-start.11
  66.3 1.0 copy-start.13
  66.8 1.0 copy-start.14
  67.3 1.0 copy-start.15
  109.2 13.1 %copy-start.8 = (f32[392,128]{1,0:T(8,128)S(1)}, f32[392,128]{1,0:T(8,128)}, u32[]{:S(2)}) copy-start(f32[392,128]{1,0:T(8,128)} %reshape.515) | copy-start | bytes 602116
  109.3 13.0 %copy-start.1 = (f32[392,512]{1,0:T(8,128)S(1)}, f32[392,512]{1,0:T(8,128)}, u32[]{:S(2)}) copy-start(f32[392,512]{1,0:T(8,128)} %convolution_add_fusion.1) | copy-start | bytes 2408452
  115.4 16.3 %all-to-all-start.2 = ((f32[64,1,128]{2,1,0:T(1,128)}), f32[64,1,128]{2,1,0:T(1,128)S(1)}, u32[]{:S(2)}, u32[]{:S(2)}) async-start(f32[64,1,128]{2,1,0:T(1,128)} %broadcast_in_dim.40), calls=%async_computation.2 | async-start | bytes 65536 | tf_op jit(solution)/shard_map/all_to_all | solution.py:78
  125.2 53.1 %copy-start.16 = (f32[2,3,3,512]{3,0,2,1:T(2,128)S(1)}, f32[2,3,3,512]{3,0,2,1:T(2,128)}, u32[]{:S(2)}) copy-start(f32[2,3,3,512]{3,0,2,1:T(2,128)} %param.7) | copy-start | bytes 110596
  131.6 34.3 %all-to-all-start = ((f32[8,196,128]{2,1,0:T(8,128)}), f32[8,196,128]{2,1,0:T(8,128)S(1)}, u32[]{:S(2)}, u32[]{:S(2)}) async-start(f32[8,196,128]{2,1,0:T(8,128)} %copy.282), calls=%async_computation | async-start | bytes 1638400 | tf_op jit(solution)/shard_map/all_to_all | solution.py:106
  167.2 9.7 %all-to-all-start.3 = ((f32[8,1,128]{2,1,0:T(1,128)}), f32[8,1,128]{2,1,0:T(1,128)S(1)}, u32[]{:S(2)}, u32[]{:S(2)}) async-start(f32[8,1,128]{2,1,0:T(1,128)} %broadcast_in_dim.41), calls=%async_computation.3 | async-start | bytes 8192 | tf_op jit(solution)/shard_map/all_to_all | solution.py:78
